TPU v7x, 32 devices: a whole 2x2x4 slice. The times are simulated.
32 devices in a mesh: section: 2 (over core), expert: 16 (over z, y, x).
Axes of the slice: x: 2, y: 2, z: 4, core: 2. Of those that a mesh axis runs over, the one named last changes fastest.
Arguments:
- fwd_states: bfloat16 [2, 2048, 2048], P('section', 'expert'), may hold values from -16 to 16
- fwd_routes: int32 [2, 2048, 2], P('section', 'expert'), may hold values from 0 to 15, all different within a row; in each aligned block of 128 rows (0 to 127, 128 to 255, ..., all dimensions but the last counted through in order) at most 20 rows name the same one
- bwd_states: bfloat16 [2, 2048, 2048], P('section', 'expert'), may hold values from -16 to 16
- bwd_routes: int32 [2, 2048, 2], P('section', 'expert'), may hold values from 0 to 15, all different within a row; in each aligned block of 128 rows (0 to 127, 128 to 255, ..., all dimensions but the last counted through in order) at most 20 rows name the same one
- bwd_cot: bfloat16 [2, 2048, 2048], P('section', 'expert'), may hold values from -1.5 to 1.5
- w_in: bfloat16 [16, 512, 2048], P('expert', 'section'), may hold values from -0.125 to 0.125
- w_out: bfloat16 [16, 512, 2048], P('expert', 'section'), may hold values from -0.25 to 0.25
Outputs:
- next_states: bfloat16 [2, 2048, 2048], P('section', 'expert')
- prev_cot: bfloat16 [2, 2048, 2048], P('section', 'expert')
- grad_w_in: float32 [16, 512, 2048], P('expert', 'section')
- grad_w_out: float32 [16, 512, 2048], P('expert', 'section')
Inputs may be any that keep to these rules, and one draw needn't show every extreme that they name: `fwd_routes`: each row names 2 different experts; in each aligned block of 128 rows (the rows of one device in one section) no expert is named by more than 20 rows, and in some block one expert is named by exactly 20 rows. `bwd_routes`: each row names 2 different experts; in each aligned block of 128 rows (the rows of one device in one section) no expert is named by more than 20 rows, and in some block one expert is named by exactly 20 rows.
All inputs are finite; a program needn't handle non-finite values.
Results may differ from a plain program's by a relative error of at most 0.012.
Values may be sent and summed in bfloat16 or wider, within the bound.
A program may use at most 64 MiB of HBM per device.

v0:
```python
import functools
import math
import jax
import jax.numpy as jnp
from jax import lax
from jax.experimental import pallas as pl
from jax.experimental.pallas import tpu as pltpu
from jax.sharding import PartitionSpec as P

EPSILON = 1e-06
CHUNKS = 4
ROWS = 16
F32, BF16 = jnp.float32, jnp.bfloat16
NT = (((1,), (1,)), ((), ()))
NN = (((1,), (0,)), ((), ()))
TN = (((0,), (0,)), ((), ()))
FWD, BWD, COT = 0, 1, 2


def mm(a, b, dims):
    return lax.dot_general(a, b, dims, preferred_element_type=F32)


def kernel(
    experts, sections, main, tail,
    xf_hbm, rf_hbm, xb_hbm, rb_hbm, g_hbm, win_hbm, wout_hbm,
    next_ref, prev_ref, gin_ref, gout_ref,
    xf_ref, rf_ref, xb_ref, rb_ref, g_ref,
    send, recv, home, back, u_tok, far_tok, far_routes, w_in, w_out, rows_u, rows_g, rows_f, act, slope, hid, side, front,
    tail_rows, part_in, part_out, table, spread, near_sum, far_send, far_part, result,
    loaded, tok_send, tok_recv, route_send, route_recv, near_send, near_recv, home_near, home_far, back_recv,
    cross_send, cross_recv, w_send, w_recv, p_send, p_recv, s_send, s_recv,
):
    tokens, depth = xf_hbm.shape
    wide = depth // CHUNKS
    blocks = main // ROWS
    q = ROWS // tail if tail else wide // 256
    thin = wide // q
    own_h = win_hbm.shape[0]
    near = experts // 2
    quarter = experts // 4
    span = near * ROWS
    n_main = experts * main
    me = lax.axis_index("expert")
    sec = lax.axis_index("section")
    half = me // near
    place = lax.rem(me, near)
    column = lax.rem(me, quarter)
    layer = place // quarter
    outward = jnp.where(half == 0, 1 - layer, layer)
    inner = outward == 0
    hub_layer = 1 + half
    my_relay = (2 - half) * quarter + column

    def source(r):
        return (2 - half + r * (1 - 2 * half)) * quarter + column

    def cols(c):
        return pl.ds(pl.multiple_of(c * wide, wide), wide)

    def strip(c, j):
        return pl.ds(pl.multiple_of(c * wide + j * thin, thin), thin)

    loads = [
        pltpu.make_async_copy(src, dst, loaded.at[i])
        for i, (src, dst) in enumerate(
            ((g_hbm, g_ref), (rb_hbm, rb_ref), (rf_hbm, rf_ref), (xb_hbm, xb_ref), (xf_hbm, xf_ref))
        )
    ]
    for load in loads:
        load.start()

    barrier = pltpu.get_barrier_semaphore()

    @pl.loop(1, near)
    def _(k):
        pl.semaphore_signal(barrier, inc=1, device_id={"expert": half * near + lax.rem(place + k, near)})

    @pl.loop(1, sections)
    def _(k):
        pl.semaphore_signal(barrier, inc=1, device_id={"section": lax.rem(sec + k, sections)})

    pl.semaphore_signal(barrier, inc=1, device_id={"expert": my_relay})

    @pl.when(inner)
    def _():
        pl.semaphore_signal(barrier, inc=1, device_id={"expert": source(1)})

    own_rows = pl.ds(pl.multiple_of(sec * own_h, own_h), own_h)
    weights = ((win_hbm, w_in), (wout_hbm, w_out))
    for i, (src, dst) in enumerate(weights):
        pltpu.make_async_copy(src, dst.at[own_rows], w_recv.at[i]).start()

    def routing(which, routes):
        lane_e = lax.broadcasted_iota(jnp.int32, (tokens, near), 1).astype(F32)
        row = lax.broadcasted_iota(jnp.int32, (tokens, tokens), 0)
        col = lax.broadcasted_iota(jnp.int32, (tokens, tokens), 1)
        names = (routes - half * near).astype(F32).astype(BF16)
        columns = mm((row == col).astype(F32).astype(BF16), names, NT)
        named = [columns[:, k : k + 1] for k in range(routes.shape[0])]
        hits = [(i == lane_e).astype(F32) for i in named]
        counts = functools.reduce(jnp.add, hits)
        rank = mm((row > col).astype(F32).astype(BF16), counts.astype(BF16), NN)
        spots = []
        for i, h in zip(named, hits):
            p = jnp.sum(h * rank, axis=1, keepdims=True)
            slot = jnp.full_like(p, -1.0)
            for b in range(blocks):
                low = b * ROWS
                slot = jnp.where((p >= low) & (p < low + ROWS), b * span + i * ROWS + (p - low), slot)
            spots.append((i, p, slot))
        lanes = table.shape[-1]
        lane = lax.broadcasted_iota(jnp.int32, (tokens, lanes), 1).astype(F32)
        for j in range(table.shape[1]):
            hit = jnp.zeros((tokens, lanes), F32)
            for i, p, slot in spots:
                if tail:
                    slot = jnp.where(p >= main, blocks * span + i * ROWS + j * tail + (p - main), slot)
                slot = jnp.where((i >= 0) & (i < near), slot, -1.0)
                hit = jnp.where(lane == slot, 1.0, hit)
            table[which, j] = hit.astype(BF16)

    def normalize(x_ref, which):
        @pl.loop(0, tokens // 16)
        def _(i):
            rows = pl.ds(pl.multiple_of(i * 16, 16), 16)
            x = x_ref[rows, :].astype(F32)
            inv = lax.rsqrt(jnp.mean(x * x, axis=-1, keepdims=True) + EPSILON)
            u_tok[which, rows, :] = (x * inv).astype(BF16)

    def picks(which, j):
        return table[which, j if tail else 0]

    def dispatch(stream, k, c, src):
        which = min(stream, 1) * 3 + k
        total = None
        for j in range(q):
            out = mm(picks(which, j), src[:, strip(c, j)], TN)
            for b in range(blocks):
                send[stream, k, :, c, :, b * wide + j * thin : b * wide + (j + 1) * thin] = (
                    out[b * span : (b + 1) * span].astype(BF16).reshape(near, ROWS, thin)
                )
            if tail:
                rest = out[blocks * span :]
                total = rest if total is None else total + rest
        if tail:
            send[stream, k, :, c, :, blocks * wide :] = total.astype(BF16).reshape(near, ROWS, thin)

    def to_near(stream, k, c, origin):
        pltpu.make_async_copy(
            send.at[stream, k, place, c], recv.at[stream, c, origin], near_recv.at[stream, c]
        ).start()

        @pl.loop(1, near)
        def _(i):
            spot = lax.rem(place + i, near)
            pltpu.make_async_remote_copy(
                src_ref=send.at[stream, k, spot, c],
                dst_ref=recv.at[stream, c, origin],
                send_sem=near_send.at[stream, k],
                recv_sem=near_recv.at[stream, c],
                device_id={"expert": half * near + spot},
            ).start()

    def own_tokens(stream, src):
        @pl.loop(0, CHUNKS)
        def _(c):
            dispatch(stream, 0, c, src)
            to_near(stream, 0, c, me)

    def to_relay(stream, src):
        @pl.loop(0, CHUNKS)
        def _(c):
            pltpu.make_async_remote_copy(
                src_ref=src.at[:, cols(c)], dst_ref=far_tok.at[stream, outward, :, cols(c)],
                send_sem=tok_send.at[stream], recv_sem=tok_recv.at[stream, outward, c],
                device_id={"expert": my_relay},
            ).start()

    def routes_to_relay(micro, src):
        pltpu.make_async_remote_copy(
            src_ref=src, dst_ref=far_routes.at[micro, outward],
            send_sem=route_send.at[micro], recv_sem=route_recv.at[micro, outward],
            device_id={"expert": my_relay},
        ).start()

    def relay_routes(micro):
        @pl.loop(0, 2)
        def _(r):
            mine = far_routes.at[micro, r]
            pltpu.make_async_copy(mine, mine, route_recv.at[micro, r]).wait()
            routing(micro * 3 + 1 + r, far_routes[micro, r])

    def relay(stream, r, low, high):
        @pl.loop(low, high)
        def _(c):
            block = far_tok.at[stream, r, :, cols(c)]
            pltpu.make_async_copy(block, block, tok_recv.at[stream, r, c]).wait()
            dispatch(stream, 1 + r, c, far_tok.at[stream, r])
            to_near(stream, 1 + r, c, source(r))

    def contract(stream, rows_ref, weight, total, low=0, high=CHUNKS):
        if low == 0:
            total[...] = jnp.zeros_like(total)

        @pl.loop(low, high)
        def _(c):
            buf = recv.at[stream, c]
            pltpu.make_async_copy(buf, buf, near_recv.at[stream, c]).wait()
            for b in range(blocks):
                rows_ref[b * experts * ROWS : (b + 1) * experts * ROWS, cols(c)] = buf[
                    :, :, b * wide : (b + 1) * wide
                ].reshape(experts * ROWS, wide)
            if tail:
                for h in range(2):
                    packed = buf[h * near : (h + 1) * near, :, blocks * wide :].reshape(span, thin)
                    for j in range(q):
                        rows_ref[n_main + h * near * tail : n_main + (h + 1) * near * tail, strip(c, j)] = mm(
                            spread[j], packed, NN
                        ).astype(BF16)
            total[...] += mm(rows_ref[:, cols(c)], weight[:, cols(c)], NT)

    def expand(act_rows, weight, slot):
        @pl.loop(0, CHUNKS)
        def _(c):
            buf = home.at[slot, c]
            step = min(512, wide)
            for i in range(wide // step):
                part = pl.ds(pl.multiple_of(c * wide + i * step, step), step)
                out = mm(act_rows[...], weight[:, part], NN).astype(BF16)
                for b in range(blocks):
                    buf[:, :, b * wide + i * step : b * wide + (i + 1) * step] = out[
                        b * experts * ROWS : (b + 1) * experts * ROWS
                    ].reshape(experts, ROWS, step)
                if tail:
                    tail_rows[:, i * step : (i + 1) * step] = out[n_main:]
            if tail:
                for h in range(2):
                    total = None
                    for j in range(q):
                        block = tail_rows[h * near * tail : (h + 1) * near * tail, j * thin : (j + 1) * thin]
                        moved = mm(spread[j], block, TN)
                        total = moved if total is None else total + moved
                    buf[h * near : (h + 1) * near, :, blocks * wide :] = total.astype(BF16).reshape(
                        near, ROWS, thin
                    )
            give_back(slot, c)

    def give_back(slot, c):
        for r in range(2):
            @pl.loop(0, quarter)
            def _(k):
                col = lax.rem(column + k, quarter)
                hub = hub_layer * quarter + col
                block = home.at[slot, c, (2 - half + r * (1 - 2 * half)) * quarter + col]
                there = back.at[slot, c, 1 + r, place]

                @pl.when(hub == me)
                def _():
                    pltpu.make_async_copy(block, there, back_recv.at[slot, c, 1 + r]).start()

                @pl.when(hub != me)
                def _():
                    pltpu.make_async_remote_copy(
                        src_ref=block, dst_ref=there,
                        send_sem=home_far.at[slot], recv_sem=back_recv.at[slot, c, 1 + r],
                        device_id={"expert": hub},
                    ).start()

        pltpu.make_async_copy(
            home.at[slot, c, me], back.at[slot, c, 0, place], back_recv.at[slot, c, 0]
        ).start()

        @pl.loop(1, near)
        def _(k):
            peer = half * near + lax.rem(place + k, near)
            pltpu.make_async_remote_copy(
                src_ref=home.at[slot, c, peer], dst_ref=back.at[slot, c, 0, place],
                send_sem=home_near.at[slot], recv_sem=back_recv.at[slot, c, 0],
                device_id={"expert": peer},
            ).start()

    def combine(slot, c, k, out_ref):
        buf = back.at[slot, c, k]
        pltpu.make_async_copy(buf, buf, back_recv.at[slot, c, k]).wait()
        for j in range(q):
            pieces = [
                buf[:, :, b * wide + j * thin : b * wide + (j + 1) * thin].reshape(span, thin) for b in range(blocks)
            ]
            if tail:
                pieces.append(buf[:, :, blocks * wide :].reshape(span, thin))
            out = mm(picks(slot * 3 + k, j), jnp.concatenate(pieces, axis=0), NN)
            out_ref[:, strip(c, j)] = out.astype(out_ref.dtype)

    def cross(slot, low, high):
        @pl.loop(low, high)
        def _(c):
            for r in (1, 0):
                combine(slot, c, 1 + r, far_send.at[slot, r])
                pltpu.make_async_remote_copy(
                    src_ref=far_send.at[slot, r, :, cols(c)], dst_ref=far_part.at[slot, :, cols(c)],
                    send_sem=cross_send.at[slot, r], recv_sem=cross_recv.at[slot, c],
                    device_id={"expert": source(r)},
                ).start()

    def own_sum(slot):
        @pl.loop(0, CHUNKS)
        def _(c):
            combine(slot, c, 0, near_sum.at[slot])

    def crossed(slot, c):
        block = far_part.at[slot, :, cols(c)]
        pltpu.make_async_copy(block, block, cross_recv.at[slot, c]).wait()

    def weight_terms(left, right, part):
        step = min(512, depth)

        @pl.loop(0, depth // step)
        def _(j):
            sl = pl.ds(pl.multiple_of(j * step, step), step)
            part[:, sl] = mm(left[...], right[:, sl], TN).astype(BF16)

    def share(i, part, out):
        pltpu.make_async_copy(part.at[own_rows], out.at[sec], p_recv.at[i]).start()

        @pl.loop(1, sections)
        def _(k):
            peer = lax.rem(sec + k, sections)
            pltpu.make_async_remote_copy(
                src_ref=part.at[pl.ds(pl.multiple_of(peer * own_h, own_h), own_h)],
                dst_ref=out.at[sec],
                send_sem=p_send.at[i], recv_sem=p_recv.at[i],
                device_id={"section": peer},
            ).start()

    outer = jnp.logical_not(inner)
    for load in loads[:3]:
        load.wait()
    pl.semaphore_wait(barrier, near + sections - 1 + jnp.where(inner, 1, 0))
    routes_to_relay(1, rb_ref)
    routes_to_relay(0, rf_ref)

    @pl.when(outer)
    def _():
        to_relay(COT, g_ref)

    for i, (src, dst) in enumerate(weights):
        @pl.loop(1, sections)
        def _(k):
            pltpu.make_async_remote_copy(
                src_ref=src, dst_ref=dst.at[own_rows],
                send_sem=w_send.at[i], recv_sem=w_recv.at[i],
                device_id={"section": lax.rem(sec + k, sections)},
            ).start()

    loads[3].wait()
    normalize(xb_ref, 1)

    @pl.when(outer)
    def _():
        to_relay(BWD, u_tok.at[1])

    @pl.when(inner)
    def _():
        to_relay(COT, g_ref)
        to_relay(BWD, u_tok.at[1])

    routing(3, rb_ref[...])
    own_tokens(COT, g_ref)
    own_tokens(BWD, u_tok.at[1])
    loads[4].wait()
    normalize(xf_ref, 0)
    routing(0, rf_ref[...])

    if tail:
        shape = (near * tail, span)
        row = lax.broadcasted_iota(jnp.int32, shape, 0).astype(F32)
        col = lax.broadcasted_iota(jnp.int32, shape, 1).astype(F32)
        start = row + jnp.floor((row + 0.5) * (1.0 / tail)) * (ROWS - tail)
        for j in range(q):
            spread[j] = jnp.where(col == start + j * tail, 1.0, 0.0).astype(BF16)

    for i, dst in enumerate((w_in, w_out)):
        pltpu.make_async_copy(dst, dst, w_recv.at[i]).wait()

    split = CHUNKS // 2
    last = CHUNKS - 1

    @pl.when(outer)
    def _():
        own_tokens(FWD, u_tok.at[0])

    @pl.when(inner)
    def _():
        to_relay(FWD, u_tok.at[0])
        relay_routes(1)
        relay(COT, 1, 0, CHUNKS)
        relay(BWD, 1, 0, CHUNKS)
        relay_routes(0)
        relay(COT, 0, 0, CHUNKS)
        relay(BWD, 0, 0, split)

    contract(COT, rows_g, w_out, slope)

    @pl.when(inner)
    def _():
        relay(BWD, 0, split, CHUNKS)
        own_tokens(FWD, u_tok.at[0])

    contract(BWD, rows_u, w_in, act, 0, last)

    @pl.when(outer)
    def _():
        to_relay(FWD, u_tok.at[0])

    contract(BWD, rows_u, w_in, act, last, CHUNKS)
    sigma = jax.nn.sigmoid(act[...])
    hid[...] = (slope[...] * (sigma * (1.0 + act[...] * (1.0 - sigma)))).astype(BF16)
    expand(hid, w_in, 1)
    side[...] = jax.nn.silu(act[...]).astype(BF16)

    @pl.when(inner)
    def _():
        relay(FWD, 1, 0, CHUNKS)
        relay(FWD, 0, 0, last)
        cross(1, 0, 1)
        relay(FWD, 0, last, CHUNKS)
        cross(1, 1, split)

    contract(FWD, rows_f, w_in, act)
    front[...] = jax.nn.silu(act[...]).astype(BF16)

    @pl.when(inner)
    def _():
        cross(1, split, last)

    expand(front, w_out, 0)

    @pl.when(inner)
    def _():
        cross(1, last, CHUNKS)

    weight_terms(hid, rows_u, part_in)
    share(0, part_in, gin_ref)
    weight_terms(side, rows_g, part_out)
    share(1, part_out, gout_ref)
    own_sum(1)

    @pl.when(inner)
    def _():
        cross(0, 0, CHUNKS)

    for c in range(CHUNKS):
        crossed(1, c)

    @pl.loop(0, tokens // 16)
    def _(i):
        rows = pl.ds(pl.multiple_of(i * 16, 16), 16)
        x = xb_ref[rows, :].astype(F32)
        total = near_sum[1, rows, :] + far_part[1, rows, :].astype(F32)
        inv = lax.rsqrt(jnp.mean(x * x, axis=-1, keepdims=True) + EPSILON)
        proj = jnp.mean(total * x, axis=-1, keepdims=True)
        grad = g_ref[rows, :].astype(F32) + inv * total - x * (inv * inv * inv) * proj
        result[1, rows, :] = grad.astype(BF16)

    to_prev = pltpu.make_async_remote_copy(
        src_ref=result.at[1], dst_ref=prev_ref, send_sem=s_send.at[1], recv_sem=s_recv.at[1],
        device_id={"section": lax.rem(sec + sections - 1, sections)},
    )
    to_prev.start()
    own_sum(0)

    @pl.loop(0, CHUNKS)
    def _(c):
        crossed(0, c)

        @pl.loop(0, tokens // 16)
        def _(i):
            rows = pl.ds(pl.multiple_of(i * 16, 16), 16)
            total = near_sum[0, rows, cols(c)] + far_part[0, rows, cols(c)].astype(F32)
            result[0, rows, cols(c)] = (xf_ref[rows, cols(c)].astype(F32) + total).astype(BF16)

        pltpu.make_async_remote_copy(
            src_ref=result.at[0, :, cols(c)], dst_ref=next_ref.at[:, cols(c)],
            send_sem=s_send.at[0], recv_sem=s_recv.at[0],
            device_id={"section": lax.rem(sec + 1, sections)},
        ).start()

    for i, (src, out) in enumerate(((win_hbm, gin_ref), (wout_hbm, gout_ref))):
        pltpu.make_async_copy(out, out, p_recv.at[i]).wait()

        @pl.loop(1, sections)
        def _(k):
            pltpu.make_async_copy(src, src, w_send.at[i]).wait()
            pltpu.make_async_copy(src, src, p_send.at[i]).wait()

    def drain(ref, sem):
        pltpu.make_async_copy(ref, ref, sem).wait()

    for stream in range(3):
        drain(g_ref, tok_send.at[stream])
        drain(send.at[0, 0, pl.ds(0, near - 1)], near_send.at[stream, 0])

    for micro, src in enumerate((rf_ref, rb_ref)):
        drain(src, route_send.at[micro])
    for slot in range(2):
        drain(home.at[0, :, pl.ds(0, near - 1)], home_near.at[slot])

    @pl.when(inner)
    def _():
        for stream in range(3):
            for r in range(2):
                drain(send.at[0, 0, pl.ds(0, near - 1)], near_send.at[stream, 1 + r])
        for slot in range(2):
            drain(home.at[0, :, pl.ds(0, near - 2)], home_far.at[slot])
            for r in range(2):
                drain(far_send.at[slot, r], cross_send.at[slot, r])

    @pl.when(jnp.logical_not(inner))
    def _():
        for slot in range(2):
            drain(home.at[0, :, pl.ds(0, near)], home_far.at[slot])

    to_prev.wait()
    drain(next_ref, s_recv.at[0])
    drain(result.at[0], s_send.at[0])


def per_device(fwd_states, fwd_routes, bwd_states, bwd_routes, bwd_cot, w_in, w_out):
    experts, sections = lax.axis_size("expert"), lax.axis_size("section")
    _, tokens, depth = fwd_states.shape
    top = fwd_routes.shape[2]
    own_h = w_in.shape[1]
    full_h = own_h * sections
    cap = max(2, (5 * tokens * top + 4 * experts - 1) // (4 * experts))
    main, tail = cap // ROWS * ROWS, cap % ROWS
    tail = next(t for t in (0, 2, 4, 8, 16) if t >= tail)
    main, tail = main + tail // ROWS * ROWS, tail % ROWS
    rows = experts * (main + tail)
    near = experts // 2
    wide = depth // CHUNKS
    q = ROWS // tail if tail else wide // 256
    thin = wide // q
    blocks = main // ROWS
    lanes = blocks * wide + (thin if tail else 0)
    picked = (blocks + (1 if tail else 0)) * near * ROWS
    buffers = [
        pltpu.VMEM((tokens, depth), BF16),
        pltpu.VMEM((top, tokens), jnp.int32),
        pltpu.VMEM((tokens, depth), BF16),
        pltpu.VMEM((top, tokens), jnp.int32),
        pltpu.VMEM((tokens, depth), BF16),
        pltpu.VMEM((3, 3, near, CHUNKS, ROWS, lanes), BF16),
        pltpu.VMEM((3, CHUNKS, experts, ROWS, lanes), BF16),
        pltpu.VMEM((2, CHUNKS, experts, ROWS, lanes), BF16),
        pltpu.VMEM((2, CHUNKS, 3, near, ROWS, lanes), BF16),
        pltpu.VMEM((2, tokens, depth), BF16),
        pltpu.VMEM((3, 2, tokens, depth), BF16),
        pltpu.VMEM((2, 2, top, tokens), jnp.int32),
        pltpu.VMEM((full_h, depth), BF16),
        pltpu.VMEM((full_h, depth), BF16),
        pltpu.VMEM((rows, depth), BF16),
        pltpu.VMEM((rows, depth), BF16),
        pltpu.VMEM((rows, depth), BF16),
        pltpu.VMEM((rows, full_h), F32),
        pltpu.VMEM((rows, full_h), F32),
        pltpu.VMEM((rows, full_h), BF16),
        pltpu.VMEM((rows, full_h), BF16),
        pltpu.VMEM((rows, full_h), BF16),
        pltpu.VMEM((max(ROWS, experts * tail), wide), BF16),
        pltpu.VMEM((full_h, depth), BF16),
        pltpu.VMEM((full_h, depth), BF16),
        pltpu.VMEM((6, q if tail else 1, tokens, picked), BF16),
        pltpu.VMEM((q, max(ROWS, near * tail), near * ROWS), BF16),
        pltpu.VMEM((2, tokens, depth), F32),
        pltpu.VMEM((2, 2, tokens, depth), BF16),
        pltpu.VMEM((2, tokens, depth), BF16),
        pltpu.VMEM((2, tokens, depth), BF16),
    ]
    grant = sum(math.prod(b.shape) * jnp.dtype(b.dtype).itemsize for b in buffers) + 3 * 1024 * 1024
    anywhere = pl.BlockSpec(memory_space=pl.ANY)
    dma = pltpu.SemaphoreType.DMA
    states = jax.ShapeDtypeStruct((tokens, depth), BF16)
    parts = jax.ShapeDtypeStruct((sections, own_h, depth), BF16)
    operands = (fwd_states[0], fwd_routes[0].T, bwd_states[0], bwd_routes[0].T, bwd_cot[0], w_in[0], w_out[0])
    next_states, prev_cot, part_in, part_out = pl.pallas_call(
        functools.partial(kernel, experts, sections, main, tail),
        out_shape=(states, states, parts, parts),
        in_specs=[pl.BlockSpec(memory_space=pltpu.HBM)] * 7,
        out_specs=(anywhere,) * 4,
        scratch_shapes=[
            *buffers,
            dma((5,)), dma((3,)), dma((3, 2, CHUNKS)), dma((2,)), dma((2, 2)), dma((3, 3)), dma((3, CHUNKS)),
            dma((2,)), dma((2,)), dma((2, CHUNKS, 3)), dma((2, 2)), dma((2, CHUNKS)),
            dma((2,)), dma((2,)), dma((2,)), dma((2,)), dma((2,)), dma((2,)),
        ],
        compiler_params=pltpu.CompilerParams(
            collective_id=0, has_side_effects=True, vmem_limit_bytes=grant
        ),
    )(*(pltpu.with_memory_space_constraint(v, pltpu.HBM) for v in operands))
    grad_in = jnp.sum(part_in.astype(F32), axis=0)
    grad_out = jnp.sum(part_out.astype(F32), axis=0)
    return next_states[None], prev_cot[None], grad_in[None], grad_out[None]


def solution(mesh):
    in_specs = (P("section", "expert", None),) * 5 + (P("expert", "section", None),) * 2
    out_specs = (P("section", "expert", None),) * 2 + (P("expert", "section", None),) * 2
    return jax.shard_map(
        per_device, mesh=mesh, in_specs=in_specs, out_specs=out_specs, check_vma=False
    )
```

profile of v0, /device:TPU:0, one launch (start us, length us, event | category | flops | bytes accessed | tf_op | source)
XLA Modules:
  0.0 130.4 jit_solution(7655227844367056429)
XLA Ops:
  0.6 125.4 %shard_map.102 = (bf16[128,2048]{1,0:T(8,128)(2,1)S(1)}, bf16[128,2048]{1,0:T(8,128)(2,1)S(1)}, bf16[2,256,2048]{2,1,0:T(8,128)(2,1)S(1)}, bf16[2,256,2048]{2,1,0:T(8,128)(2,1)S(1)}) custom-call(bf16[128,2048]{1,0:T(8,128)(2,1)} %bitcast.21, s32[2,128]{1,0:T(2,128)} %bitcast.24, bf16[128,2048]{1,0:T(8,128)(2,1)} %bitcast.22, s32[2,128]{1,0:T(2,128)} %bitcast.25, ...), custom_call_target="tpu_custom_call" | custom-call | tf_op jit(solution)/shard_map/pallas_call | solution.py:586
  126.0 2.9 %convert_reduce_fusion = (f32[256,2048]{1,0:T(8,128)}, f32[256,2048]{1,0:T(8,128)}) fusion(bf16[2,256,2048]{2,1,0:T(8,128)(2,1)S(1)} %get-tuple-element.11, bf16[2,256,2048]{2,1,0:T(8,128)(2,1)S(1)} %get-tuple-element.10), kind=kLoop, calls=%fused_computation | loop fusion | flops 3145728 | bytes 8388608 | tf_op jit(solution)/shard_map/reduce_sum | solution.py:602
  128.9 0.8 copy.13
  129.6 0.8 copy.14
where the time goes:
time: 131 us; the launch traced here: 130 us
  Pallas kernels  125 us (95%)
  other arithmetic  2.85 us (2%)
  local copies, waits for them, and re-layouts  1.59 us (1%)
    pallas_call x1, Pallas kernels, per_device(): pl.pallas_call(functools.partial(kernel, experts, sections, main, tail),...  125 us
    reduce_sum x1, other arithmetic, per_device(): grad_out = jnp.sum(part_out.astype(F32), axis=0)  2.85 us

commit v1 on v0

--- a/solution.py
+++ b/solution.py
@@ -87,9 +87,6 @@
         pl.semaphore_signal(barrier, inc=1, device_id={"expert": source(1)})
 
     own_rows = pl.ds(pl.multiple_of(sec * own_h, own_h), own_h)
-    weights = ((win_hbm, w_in), (wout_hbm, w_out))
-    for i, (src, dst) in enumerate(weights):
-        pltpu.make_async_copy(src, dst.at[own_rows], w_recv.at[i]).start()
 
     def routing(which, routes):
         lane_e = lax.broadcasted_iota(jnp.int32, (tokens, near), 1).astype(F32)
@@ -244,9 +241,9 @@
                     buf[h * near : (h + 1) * near, :, blocks * wide :] = total.astype(BF16).reshape(
                         near, ROWS, thin
                     )
-            give_back(slot, c)
-
-    def give_back(slot, c):
+            give_far(slot, c)
+
+    def give_far(slot, c):
         for r in range(2):
             @pl.loop(0, quarter)
             def _(k):
@@ -267,18 +264,21 @@
                         device_id={"expert": hub},
                     ).start()
 
-        pltpu.make_async_copy(
-            home.at[slot, c, me], back.at[slot, c, 0, place], back_recv.at[slot, c, 0]
-        ).start()
-
-        @pl.loop(1, near)
-        def _(k):
-            peer = half * near + lax.rem(place + k, near)
-            pltpu.make_async_remote_copy(
-                src_ref=home.at[slot, c, peer], dst_ref=back.at[slot, c, 0, place],
-                send_sem=home_near.at[slot], recv_sem=back_recv.at[slot, c, 0],
-                device_id={"expert": peer},
+    def give_near(slot):
+        @pl.loop(0, CHUNKS)
+        def _(c):
+            pltpu.make_async_copy(
+                home.at[slot, c, me], back.at[slot, c, 0, place], back_recv.at[slot, c, 0]
             ).start()
+
+            @pl.loop(1, near)
+            def _(k):
+                peer = half * near + lax.rem(place + k, near)
+                pltpu.make_async_remote_copy(
+                    src_ref=home.at[slot, c, peer], dst_ref=back.at[slot, c, 0, place],
+                    send_sem=home_near.at[slot], recv_sem=back_recv.at[slot, c, 0],
+                    device_id={"expert": peer},
+                ).start()
 
     def combine(slot, c, k, out_ref):
         buf = back.at[slot, c, k]
@@ -292,16 +292,18 @@
             out = mm(picks(slot * 3 + k, j), jnp.concatenate(pieces, axis=0), NN)
             out_ref[:, strip(c, j)] = out.astype(out_ref.dtype)
 
-    def cross(slot, low, high):
+    def cross(slot, c, r):
+        combine(slot, c, 1 + r, far_send.at[slot, r])
+        pltpu.make_async_remote_copy(
+            src_ref=far_send.at[slot, r, :, cols(c)], dst_ref=far_part.at[slot, :, cols(c)],
+            send_sem=cross_send.at[slot, r], recv_sem=cross_recv.at[slot, c],
+            device_id={"expert": source(r)},
+        ).start()
+
+    def cross_range(slot, r, low, high):
         @pl.loop(low, high)
         def _(c):
-            for r in (1, 0):
-                combine(slot, c, 1 + r, far_send.at[slot, r])
-                pltpu.make_async_remote_copy(
-                    src_ref=far_send.at[slot, r, :, cols(c)], dst_ref=far_part.at[slot, :, cols(c)],
-                    send_sem=cross_send.at[slot, r], recv_sem=cross_recv.at[slot, c],
-                    device_id={"expert": source(r)},
-                ).start()
+            cross(slot, c, r)
 
     def own_sum(slot):
         @pl.loop(0, CHUNKS)
@@ -344,7 +346,28 @@
     def _():
         to_relay(COT, g_ref)
 
-    for i, (src, dst) in enumerate(weights):
+    loads[3].wait()
+    normalize(xb_ref, 1)
+
+    @pl.when(outer)
+    def _():
+        to_relay(BWD, u_tok.at[1])
+
+    @pl.when(inner)
+    def _():
+        to_relay(COT, g_ref)
+        to_relay(BWD, u_tok.at[1])
+
+    routing(3, rb_ref[...])
+    own_tokens(COT, g_ref)
+    own_tokens(BWD, u_tok.at[1])
+    loads[4].wait()
+    normalize(xf_ref, 0)
+    routing(0, rf_ref[...])
+
+    for i, (src, dst) in enumerate(((win_hbm, w_in), (wout_hbm, w_out))):
+        pltpu.make_async_copy(src, dst.at[own_rows], w_recv.at[i]).start()
+
         @pl.loop(1, sections)
         def _(k):
             pltpu.make_async_remote_copy(
@@ -353,25 +376,6 @@
                 device_id={"section": lax.rem(sec + k, sections)},
             ).start()
 
-    loads[3].wait()
-    normalize(xb_ref, 1)
-
-    @pl.when(outer)
-    def _():
-        to_relay(BWD, u_tok.at[1])
-
-    @pl.when(inner)
-    def _():
-        to_relay(COT, g_ref)
-        to_relay(BWD, u_tok.at[1])
-
-    routing(3, rb_ref[...])
-    own_tokens(COT, g_ref)
-    own_tokens(BWD, u_tok.at[1])
-    loads[4].wait()
-    normalize(xf_ref, 0)
-    routing(0, rf_ref[...])
-
     if tail:
         shape = (near * tail, span)
         row = lax.broadcasted_iota(jnp.int32, shape, 0).astype(F32)
@@ -380,9 +384,6 @@
         for j in range(q):
             spread[j] = jnp.where(col == start + j * tail, 1.0, 0.0).astype(BF16)
 
-    for i, dst in enumerate((w_in, w_out)):
-        pltpu.make_async_copy(dst, dst, w_recv.at[i]).wait()
-
     split = CHUNKS // 2
     last = CHUNKS - 1
 
@@ -400,6 +401,9 @@
         relay(COT, 0, 0, CHUNKS)
         relay(BWD, 0, 0, split)
 
+    for i, dst in enumerate((w_in, w_out)):
+        pltpu.make_async_copy(dst, dst, w_recv.at[i]).wait()
+
     contract(COT, rows_g, w_out, slope)
 
     @pl.when(inner)
@@ -423,22 +427,28 @@
     def _():
         relay(FWD, 1, 0, CHUNKS)
         relay(FWD, 0, 0, last)
-        cross(1, 0, 1)
+        cross_range(1, 0, 0, 1)
         relay(FWD, 0, last, CHUNKS)
-        cross(1, 1, split)
+        give_near(1)
+        cross_range(1, 0, 1, CHUNKS)
+
+    @pl.when(outer)
+    def _():
+        give_near(1)
 
     contract(FWD, rows_f, w_in, act)
     front[...] = jax.nn.silu(act[...]).astype(BF16)
 
     @pl.when(inner)
     def _():
-        cross(1, split, last)
+        cross_range(1, 1, 0, split)
 
     expand(front, w_out, 0)
-
-    @pl.when(inner)
-    def _():
-        cross(1, last, CHUNKS)
+    give_near(0)
+
+    @pl.when(inner)
+    def _():
+        cross_range(1, 1, split, CHUNKS)
 
     weight_terms(hid, rows_u, part_in)
     share(0, part_in, gin_ref)
@@ -448,7 +458,10 @@
 
     @pl.when(inner)
     def _():
-        cross(0, 0, CHUNKS)
+        @pl.loop(0, CHUNKS)
+        def _(c):
+            cross(0, c, 1)
+            cross(0, c, 0)
 
     for c in range(CHUNKS):
         crossed(1, c)
@@ -524,6 +537,34 @@
     to_prev.wait()
     drain(next_ref, s_recv.at[0])
     drain(result.at[0], s_send.at[0])
+
+
+def finish(next_ref, prev_ref, pin_ref, pout_ref, next_out, prev_out, gin_out, gout_out, sum_in, sum_out, sems):
+    own_h = sum_in.shape[0]
+    step = own_h // 4
+    moves = [
+        pltpu.make_async_copy(next_ref, next_out, sems.at[0]),
+        pltpu.make_async_copy(prev_ref, prev_out, sems.at[1]),
+    ]
+    for move in moves:
+        move.start()
+    for i, (part, total, out) in enumerate(((pin_ref, sum_in, gin_out), (pout_ref, sum_out, gout_out))):
+        @pl.loop(0, own_h // step)
+        def _(b):
+            @pl.loop(0, step // 16)
+            def _(j):
+                rows = pl.ds(pl.multiple_of(b * step + j * 16, 16), 16)
+                total[rows, :] = functools.reduce(
+                    jnp.add, [part[k, rows, :].astype(F32) for k in range(part.shape[0])]
+                )
+
+            block = pl.ds(pl.multiple_of(b * step, step), step)
+            pltpu.make_async_copy(total.at[block], out.at[block], sems.at[2 + i]).start()
+
+    for move in moves:
+        move.wait()
+    for i, (total, out) in enumerate(((sum_in, gin_out), (sum_out, gout_out))):
+        pltpu.make_async_copy(total, out, sems.at[2 + i]).wait()
 
 
 def per_device(fwd_states, fwd_routes, bwd_states, bwd_routes, bwd_cot, w_in, w_out):
@@ -598,8 +639,15 @@
             collective_id=0, has_side_effects=True, vmem_limit_bytes=grant
         ),
     )(*(pltpu.with_memory_space_constraint(v, pltpu.HBM) for v in operands))
-    grad_in = jnp.sum(part_in.astype(F32), axis=0)
-    grad_out = jnp.sum(part_out.astype(F32), axis=0)
+    grads = jax.ShapeDtypeStruct((own_h, depth), F32)
+    next_states, prev_cot, grad_in, grad_out = pl.pallas_call(
+        finish,
+        out_shape=(states, states, grads, grads),
+        in_specs=[anywhere] * 2 + [pl.BlockSpec(memory_space=pltpu.VMEM)] * 2,
+        out_specs=(pl.BlockSpec(memory_space=pltpu.HBM),) * 4,
+        scratch_shapes=[pltpu.VMEM((own_h, depth), F32), pltpu.VMEM((own_h, depth), F32), dma((4,))],
+        compiler_params=pltpu.CompilerParams(vmem_limit_bytes=own_h * depth * 8 + 2 * 1024 * 1024),
+    )(next_states, prev_cot, part_in, part_out)
     return next_states[None], prev_cot[None], grad_in[None], grad_out[None]
 
 

time: 131 us -> 124 us (0.947)
  the two profiles are of different devices: /device:TPU:0 before, /device:TPU:15 now
where the time goes in v1:
time: 124 us; the launch traced here: 123 us
  Pallas kernels  122 us (98%)
    pallas_call x1, Pallas kernels, per_device(): pl.pallas_call(functools.partial(kernel, experts, sections, main, tail),...  120 us

profile of v1, /device:TPU:15, one launch (start us, length us, event | category | flops | bytes accessed | tf_op | source)
XLA Modules:
  0.0 122.5 jit_solution(14028860856315454826)
XLA Ops:
  0.6 119.5 %shard_map.102 = (bf16[128,2048]{1,0:T(8,128)(2,1)S(1)}, bf16[128,2048]{1,0:T(8,128)(2,1)S(1)}, bf16[2,256,2048]{2,1,0:T(8,128)(2,1)S(1)}, bf16[2,256,2048]{2,1,0:T(8,128)(2,1)S(1)}) custom-call(bf16[128,2048]{1,0:T(8,128)(2,1)} %bitcast.17, s32[2,128]{1,0:T(2,128)} %bitcast.20, bf16[128,2048]{1,0:T(8,128)(2,1)} %bitcast.18, s32[2,128]{1,0:T(2,128)} %bitcast.21, ...), custom_call_target="tpu_custom_call" | custom-call | tf_op jit(solution)/shard_map/pallas_call | solution.py:627
  120.2 2.4 %shard_map.103 = (bf16[128,2048]{1,0:T(8,128)(2,1)}, bf16[128,2048]{1,0:T(8,128)(2,1)}, f32[256,2048]{1,0:T(8,128)}, f32[256,2048]{1,0:T(8,128)}) custom-call(bf16[128,2048]{1,0:T(8,128)(2,1)S(1)} %get-tuple-element.12.next_ref, bf16[128,2048]{1,0:T(8,128)(2,1)S(1)} %get-tuple-element.13.prev_ref, bf16[2,256,2048]{2,1,0:T(8,128)(2,1)S(1)} %get-tuple-element.14.pin_ref, ...), custom_call_target="tpu_custom_call" | custom-call | tf_op jit(solution)/shard_map/pallas_call | solution.py:643

commit v2 on v1

--- a/solution.py
+++ b/solution.py
@@ -27,9 +27,9 @@
     next_ref, prev_ref, gin_ref, gout_ref,
     xf_ref, rf_ref, xb_ref, rb_ref, g_ref,
     send, recv, home, back, u_tok, far_tok, far_routes, w_in, w_out, rows_u, rows_g, rows_f, act, slope, hid, side, front,
-    tail_rows, part_in, part_out, table, spread, near_sum, far_send, far_part, result,
+    tail_rows, part_in, part_out, table, spread, near_sum, far_send, far_part, carried, result, final,
     loaded, tok_send, tok_recv, route_send, route_recv, near_send, near_recv, home_near, home_far, back_recv,
-    cross_send, cross_recv, w_send, w_recv, p_send, p_recv, s_send, s_recv,
+    cross_send, cross_recv, w_send, w_recv, p_send, p_recv, s_send, s_recv, carry_recv, final_sem,
 ):
     tokens, depth = xf_hbm.shape
     wide = depth // CHUNKS
@@ -80,7 +80,9 @@
     def _(k):
         pl.semaphore_signal(barrier, inc=1, device_id={"section": lax.rem(sec + k, sections)})
 
+    before, after = lax.rem(sec + sections - 1, sections), lax.rem(sec + 1, sections)
     pl.semaphore_signal(barrier, inc=1, device_id={"expert": my_relay})
+    pl.semaphore_signal(barrier, inc=1, device_id={"expert": my_relay, "section": before})
 
     @pl.when(inner)
     def _():
@@ -297,7 +299,7 @@
         pltpu.make_async_remote_copy(
             src_ref=far_send.at[slot, r, :, cols(c)], dst_ref=far_part.at[slot, :, cols(c)],
             send_sem=cross_send.at[slot, r], recv_sem=cross_recv.at[slot, c],
-            device_id={"expert": source(r)},
+            device_id={"expert": source(r), "section": after if slot == 0 else sec},
         ).start()
 
     def cross_range(slot, r, low, high):
@@ -336,17 +338,16 @@
             ).start()
 
     outer = jnp.logical_not(inner)
-    for load in loads[:3]:
+    pl.semaphore_wait(barrier, near + sections - 1 + jnp.where(inner, 3, 0))
+    routes_to_relay(1, rb_hbm)
+    routes_to_relay(0, rf_hbm)
+
+    @pl.when(outer)
+    def _():
+        to_relay(COT, g_hbm)
+
+    for load in loads[:4]:
         load.wait()
-    pl.semaphore_wait(barrier, near + sections - 1 + jnp.where(inner, 1, 0))
-    routes_to_relay(1, rb_ref)
-    routes_to_relay(0, rf_ref)
-
-    @pl.when(outer)
-    def _():
-        to_relay(COT, g_ref)
-
-    loads[3].wait()
     normalize(xb_ref, 1)
 
     @pl.when(outer)
@@ -474,29 +475,27 @@
         inv = lax.rsqrt(jnp.mean(x * x, axis=-1, keepdims=True) + EPSILON)
         proj = jnp.mean(total * x, axis=-1, keepdims=True)
         grad = g_ref[rows, :].astype(F32) + inv * total - x * (inv * inv * inv) * proj
-        result[1, rows, :] = grad.astype(BF16)
+        result[rows, :] = grad.astype(BF16)
 
     to_prev = pltpu.make_async_remote_copy(
-        src_ref=result.at[1], dst_ref=prev_ref, send_sem=s_send.at[1], recv_sem=s_recv.at[1],
+        src_ref=result, dst_ref=prev_ref, send_sem=s_send.at[1], recv_sem=s_recv.at[0],
         device_id={"section": lax.rem(sec + sections - 1, sections)},
     )
     to_prev.start()
-    own_sum(0)
 
     @pl.loop(0, CHUNKS)
     def _(c):
-        crossed(0, c)
+        combine(0, c, 0, near_sum.at[0])
 
         @pl.loop(0, tokens // 16)
         def _(i):
             rows = pl.ds(pl.multiple_of(i * 16, 16), 16)
-            total = near_sum[0, rows, cols(c)] + far_part[0, rows, cols(c)].astype(F32)
-            result[0, rows, cols(c)] = (xf_ref[rows, cols(c)].astype(F32) + total).astype(BF16)
+            near_sum[0, rows, cols(c)] += xf_ref[rows, cols(c)].astype(F32)
 
         pltpu.make_async_remote_copy(
-            src_ref=result.at[0, :, cols(c)], dst_ref=next_ref.at[:, cols(c)],
-            send_sem=s_send.at[0], recv_sem=s_recv.at[0],
-            device_id={"section": lax.rem(sec + 1, sections)},
+            src_ref=near_sum.at[0, :, cols(c)], dst_ref=carried.at[:, cols(c)],
+            send_sem=s_send.at[0], recv_sem=carry_recv.at[c],
+            device_id={"section": after},
         ).start()
 
     for i, (src, out) in enumerate(((win_hbm, gin_ref), (wout_hbm, gout_ref))):
@@ -526,17 +525,37 @@
                 drain(send.at[0, 0, pl.ds(0, near - 1)], near_send.at[stream, 1 + r])
         for slot in range(2):
             drain(home.at[0, :, pl.ds(0, near - 2)], home_far.at[slot])
+
+    @pl.when(jnp.logical_not(inner))
+    def _():
+        for slot in range(2):
+            drain(home.at[0, :, pl.ds(0, near)], home_far.at[slot])
+
+    to_prev.wait()
+
+    @pl.loop(0, CHUNKS)
+    def _(c):
+        moved = carried.at[:, cols(c)]
+        drain(moved, carry_recv.at[c])
+        crossed(0, c)
+
+        @pl.loop(0, tokens // 16)
+        def _(i):
+            rows = pl.ds(pl.multiple_of(i * 16, 16), 16)
+            total = carried[rows, cols(c)] + far_part[0, rows, cols(c)].astype(F32)
+            final[rows, cols(c)] = total.astype(BF16)
+
+        pltpu.make_async_copy(final.at[:, cols(c)], next_ref.at[:, cols(c)], final_sem).start()
+
+    drain(next_ref, final_sem)
+
+    drain(carried, s_send.at[0])
+
+    @pl.when(inner)
+    def _():
+        for slot in range(2):
             for r in range(2):
                 drain(far_send.at[slot, r], cross_send.at[slot, r])
-
-    @pl.when(jnp.logical_not(inner))
-    def _():
-        for slot in range(2):
-            drain(home.at[0, :, pl.ds(0, near)], home_far.at[slot])
-
-    to_prev.wait()
-    drain(next_ref, s_recv.at[0])
-    drain(result.at[0], s_send.at[0])
 
 
 def finish(next_ref, prev_ref, pin_ref, pout_ref, next_out, prev_out, gin_out, gout_out, sum_in, sum_out, sems):
@@ -616,15 +635,18 @@
         pltpu.VMEM((2, tokens, depth), F32),
         pltpu.VMEM((2, 2, tokens, depth), BF16),
         pltpu.VMEM((2, tokens, depth), BF16),
-        pltpu.VMEM((2, tokens, depth), BF16),
+        pltpu.VMEM((tokens, depth), F32),
+        pltpu.VMEM((tokens, depth), BF16),
+        pltpu.VMEM((tokens, depth), BF16),
     ]
     grant = sum(math.prod(b.shape) * jnp.dtype(b.dtype).itemsize for b in buffers) + 3 * 1024 * 1024
     anywhere = pl.BlockSpec(memory_space=pl.ANY)
     dma = pltpu.SemaphoreType.DMA
     states = jax.ShapeDtypeStruct((tokens, depth), BF16)
     parts = jax.ShapeDtypeStruct((sections, own_h, depth), BF16)
+    grads = jax.ShapeDtypeStruct((own_h, depth), F32)
     operands = (fwd_states[0], fwd_routes[0].T, bwd_states[0], bwd_routes[0].T, bwd_cot[0], w_in[0], w_out[0])
-    next_states, prev_cot, part_in, part_out = pl.pallas_call(
+    results = pl.pallas_call(
         functools.partial(kernel, experts, sections, main, tail),
         out_shape=(states, states, parts, parts),
         in_specs=[pl.BlockSpec(memory_space=pltpu.HBM)] * 7,
@@ -633,22 +655,21 @@
             *buffers,
             dma((5,)), dma((3,)), dma((3, 2, CHUNKS)), dma((2,)), dma((2, 2)), dma((3, 3)), dma((3, CHUNKS)),
             dma((2,)), dma((2,)), dma((2, CHUNKS, 3)), dma((2, 2)), dma((2, CHUNKS)),
-            dma((2,)), dma((2,)), dma((2,)), dma((2,)), dma((2,)), dma((2,)),
+            dma((2,)), dma((2,)), dma((2,)), dma((2,)), dma((2,)), dma((1,)), dma((CHUNKS,)), dma,
         ],
         compiler_params=pltpu.CompilerParams(
             collective_id=0, has_side_effects=True, vmem_limit_bytes=grant
         ),
     )(*(pltpu.with_memory_space_constraint(v, pltpu.HBM) for v in operands))
-    grads = jax.ShapeDtypeStruct((own_h, depth), F32)
-    next_states, prev_cot, grad_in, grad_out = pl.pallas_call(
+    outs = pl.pallas_call(
         finish,
         out_shape=(states, states, grads, grads),
         in_specs=[anywhere] * 2 + [pl.BlockSpec(memory_space=pltpu.VMEM)] * 2,
         out_specs=(pl.BlockSpec(memory_space=pltpu.HBM),) * 4,
         scratch_shapes=[pltpu.VMEM((own_h, depth), F32), pltpu.VMEM((own_h, depth), F32), dma((4,))],
         compiler_params=pltpu.CompilerParams(vmem_limit_bytes=own_h * depth * 8 + 2 * 1024 * 1024),
-    )(next_states, prev_cot, part_in, part_out)
-    return next_states[None], prev_cot[None], grad_in[None], grad_out[None]
+    )(*results)
+    return tuple(out[None] for out in outs)
 
 
 def solution(mesh):

time: 124 us -> 123 us (level)
  no operation moved by 1% of the time
where the time goes in v2:
time: 123 us; the launch traced here: 121 us
  Pallas kernels  121 us (98%)
    pallas_call x1, Pallas kernels, per_device(): pl.pallas_call(functools.partial(kernel, experts, sections, main, tail),...  118 us

profile of v2, /device:TPU:15, one launch (start us, length us, event | category | flops | bytes accessed | tf_op | source)
XLA Modules:
  0.0 121.4 jit_solution(8882701215384803628)
XLA Ops:
  0.6 118.4 %shard_map.102 = (bf16[128,2048]{1,0:T(8,128)(2,1)S(1)}, bf16[128,2048]{1,0:T(8,128)(2,1)S(1)}, bf16[2,256,2048]{2,1,0:T(8,128)(2,1)S(1)}, bf16[2,256,2048]{2,1,0:T(8,128)(2,1)S(1)}) custom-call(bf16[128,2048]{1,0:T(8,128)(2,1)} %bitcast.17, s32[2,128]{1,0:T(2,128)} %bitcast.20, bf16[128,2048]{1,0:T(8,128)(2,1)} %bitcast.18, s32[2,128]{1,0:T(2,128)} %bitcast.21, ...), custom_call_target="tpu_custom_call" | custom-call | tf_op jit(solution)/shard_map/pallas_call | solution.py:649
  119.0 2.4 %shard_map.103 = (bf16[128,2048]{1,0:T(8,128)(2,1)}, bf16[128,2048]{1,0:T(8,128)(2,1)}, f32[256,2048]{1,0:T(8,128)}, f32[256,2048]{1,0:T(8,128)}) custom-call(bf16[128,2048]{1,0:T(8,128)(2,1)S(1)} %get-tuple-element.12.next_ref, bf16[128,2048]{1,0:T(8,128)(2,1)S(1)} %get-tuple-element.13.prev_ref, bf16[2,256,2048]{2,1,0:T(8,128)(2,1)S(1)} %get-tuple-element.14.pin_ref, ...), custom_call_target="tpu_custom_call" | custom-call | tf_op jit(solution)/shard_map/pallas_call | solution.py:664

commit v3 on v2

--- a/solution.py
+++ b/solution.py
@@ -29,7 +29,7 @@
     send, recv, home, back, u_tok, far_tok, far_routes, w_in, w_out, rows_u, rows_g, rows_f, act, slope, hid, side, front,
     tail_rows, part_in, part_out, table, spread, near_sum, far_send, far_part, carried, result, final,
     loaded, tok_send, tok_recv, route_send, route_recv, near_send, near_recv, home_near, home_far, back_recv,
-    cross_send, cross_recv, w_send, w_recv, p_send, p_recv, s_send, s_recv, carry_recv, final_sem,
+    cross_send, cross_recv, w_send, w_recv, p_send, p_recv, s_send, s_recv, carry_recv, final_sem, go,
 ):
     tokens, depth = xf_hbm.shape
     wide = depth // CHUNKS
@@ -72,21 +72,18 @@
 
     barrier = pltpu.get_barrier_semaphore()
 
-    @pl.loop(1, near)
-    def _(k):
-        pl.semaphore_signal(barrier, inc=1, device_id={"expert": half * near + lax.rem(place + k, near)})
-
-    @pl.loop(1, sections)
-    def _(k):
-        pl.semaphore_signal(barrier, inc=1, device_id={"section": lax.rem(sec + k, sections)})
-
     before, after = lax.rem(sec + sections - 1, sections), lax.rem(sec + 1, sections)
-    pl.semaphore_signal(barrier, inc=1, device_id={"expert": my_relay})
-    pl.semaphore_signal(barrier, inc=1, device_id={"expert": my_relay, "section": before})
-
-    @pl.when(inner)
-    def _():
-        pl.semaphore_signal(barrier, inc=1, device_id={"expert": source(1)})
+    host = (me == experts - 1) & (sec == 0)
+    guest = jnp.logical_not(host)
+
+    @pl.when(inner)
+    def _():
+        for r in range(2):
+            pl.semaphore_signal(barrier, inc=1, device_id={"expert": source(r)})
+
+    @pl.when(guest)
+    def _():
+        pl.semaphore_signal(barrier, inc=1, device_id={"expert": experts - 1, "section": 0})
 
     own_rows = pl.ds(pl.multiple_of(sec * own_h, own_h), own_h)
 
@@ -338,7 +335,18 @@
             ).start()
 
     outer = jnp.logical_not(inner)
-    pl.semaphore_wait(barrier, near + sections - 1 + jnp.where(inner, 3, 0))
+    pl.semaphore_wait(barrier, 1 + jnp.where(host, experts * sections - 1, 0))
+
+    @pl.when(host)
+    def _():
+        @pl.loop(0, experts)
+        def _(e):
+            @pl.loop(0, sections)
+            def _(t):
+                @pl.when((e != me) | (t != sec))
+                def _():
+                    pl.semaphore_signal(go, inc=1, device_id={"expert": e, "section": t})
+
     routes_to_relay(1, rb_hbm)
     routes_to_relay(0, rf_hbm)
 
@@ -360,6 +368,11 @@
         to_relay(BWD, u_tok.at[1])
 
     routing(3, rb_ref[...])
+
+    @pl.when(guest)
+    def _():
+        pl.semaphore_wait(go, 1)
+
     own_tokens(COT, g_ref)
     own_tokens(BWD, u_tok.at[1])
     loads[4].wait()
@@ -655,7 +668,7 @@
             *buffers,
             dma((5,)), dma((3,)), dma((3, 2, CHUNKS)), dma((2,)), dma((2, 2)), dma((3, 3)), dma((3, CHUNKS)),
             dma((2,)), dma((2,)), dma((2, CHUNKS, 3)), dma((2, 2)), dma((2, CHUNKS)),
-            dma((2,)), dma((2,)), dma((2,)), dma((2,)), dma((2,)), dma((1,)), dma((CHUNKS,)), dma,
+            dma((2,)), dma((2,)), dma((2,)), dma((2,)), dma((2,)), dma((1,)), dma((CHUNKS,)), dma, pltpu.SemaphoreType.REGULAR,
         ],
         compiler_params=pltpu.CompilerParams(
             collective_id=0, has_side_effects=True, vmem_limit_bytes=grant

time: 123 us -> 121 us (0.984); the launches traced: 121 us -> 121 us
  no operation moved by 1% of the time
where the time goes in v3:
time: 121 us
  Pallas kernels  120 us (99%)
    pallas_call x1, Pallas kernels, per_device(): pl.pallas_call(functools.partial(kernel, experts, sections, main, tail),...  118 us

profile of v3, /device:TPU:15, one launch (start us, length us, event | category | flops | bytes accessed | tf_op | source)
XLA Modules:
  0.0 120.6 jit_solution(3764760278334454224)
XLA Ops:
  0.6 117.6 %shard_map.102 = (bf16[128,2048]{1,0:T(8,128)(2,1)S(1)}, bf16[128,2048]{1,0:T(8,128)(2,1)S(1)}, bf16[2,256,2048]{2,1,0:T(8,128)(2,1)S(1)}, bf16[2,256,2048]{2,1,0:T(8,128)(2,1)S(1)}) custom-call(bf16[128,2048]{1,0:T(8,128)(2,1)} %bitcast.17, s32[2,128]{1,0:T(2,128)} %bitcast.20, bf16[128,2048]{1,0:T(8,128)(2,1)} %bitcast.18, s32[2,128]{1,0:T(2,128)} %bitcast.21, ...), custom_call_target="tpu_custom_call" | custom-call | tf_op jit(solution)/shard_map/pallas_call | solution.py:662
  118.3 2.4 %shard_map.103 = (bf16[128,2048]{1,0:T(8,128)(2,1)}, bf16[128,2048]{1,0:T(8,128)(2,1)}, f32[256,2048]{1,0:T(8,128)}, f32[256,2048]{1,0:T(8,128)}) custom-call(bf16[128,2048]{1,0:T(8,128)(2,1)S(1)} %get-tuple-element.12.next_ref, bf16[128,2048]{1,0:T(8,128)(2,1)S(1)} %get-tuple-element.13.prev_ref, bf16[2,256,2048]{2,1,0:T(8,128)(2,1)S(1)} %get-tuple-element.14.pin_ref, ...), custom_call_target="tpu_custom_call" | custom-call | tf_op jit(solution)/shard_map/pallas_call | solution.py:677

commit v4 on v3

--- a/solution.py
+++ b/solution.py
@@ -24,12 +24,12 @@
 def kernel(
     experts, sections, main, tail,
     xf_hbm, rf_hbm, xb_hbm, rb_hbm, g_hbm, win_hbm, wout_hbm,
-    next_ref, prev_ref, gin_ref, gout_ref,
+    carried, far_next, prev_ref, gin_ref, gout_ref,
     xf_ref, rf_ref, xb_ref, rb_ref, g_ref,
     send, recv, home, back, u_tok, far_tok, far_routes, w_in, w_out, rows_u, rows_g, rows_f, act, slope, hid, side, front,
-    tail_rows, part_in, part_out, table, spread, near_sum, far_send, far_part, carried, result, final,
+    tail_rows, part_in, part_out, table, spread, near_sum, far_send, far_part, result,
     loaded, tok_send, tok_recv, route_send, route_recv, near_send, near_recv, home_near, home_far, back_recv,
-    cross_send, cross_recv, w_send, w_recv, p_send, p_recv, s_send, s_recv, carry_recv, final_sem, go,
+    cross_send, cross_recv, w_send, w_recv, p_send, p_recv, s_send, s_recv, carry_recv, go,
 ):
     tokens, depth = xf_hbm.shape
     wide = depth // CHUNKS
@@ -294,7 +294,7 @@
     def cross(slot, c, r):
         combine(slot, c, 1 + r, far_send.at[slot, r])
         pltpu.make_async_remote_copy(
-            src_ref=far_send.at[slot, r, :, cols(c)], dst_ref=far_part.at[slot, :, cols(c)],
+            src_ref=far_send.at[slot, r, :, cols(c)], dst_ref=(far_next if slot == 0 else far_part).at[:, cols(c)],
             send_sem=cross_send.at[slot, r], recv_sem=cross_recv.at[slot, c],
             device_id={"expert": source(r), "section": after if slot == 0 else sec},
         ).start()
@@ -310,7 +310,7 @@
             combine(slot, c, 0, near_sum.at[slot])
 
     def crossed(slot, c):
-        block = far_part.at[slot, :, cols(c)]
+        block = (far_next if slot == 0 else far_part).at[:, cols(c)]
         pltpu.make_async_copy(block, block, cross_recv.at[slot, c]).wait()
 
     def weight_terms(left, right, part):
@@ -484,7 +484,7 @@
     def _(i):
         rows = pl.ds(pl.multiple_of(i * 16, 16), 16)
         x = xb_ref[rows, :].astype(F32)
-        total = near_sum[1, rows, :] + far_part[1, rows, :].astype(F32)
+        total = near_sum[1, rows, :] + far_part[rows, :].astype(F32)
         inv = lax.rsqrt(jnp.mean(x * x, axis=-1, keepdims=True) + EPSILON)
         proj = jnp.mean(total * x, axis=-1, keepdims=True)
         grad = g_ref[rows, :].astype(F32) + inv * total - x * (inv * inv * inv) * proj
@@ -546,21 +546,10 @@
 
     to_prev.wait()
 
-    @pl.loop(0, CHUNKS)
-    def _(c):
-        moved = carried.at[:, cols(c)]
-        drain(moved, carry_recv.at[c])
+    for c in range(CHUNKS):
+        drain(carried.at[:, cols(c)], carry_recv.at[c])
+    for c in range(CHUNKS):
         crossed(0, c)
-
-        @pl.loop(0, tokens // 16)
-        def _(i):
-            rows = pl.ds(pl.multiple_of(i * 16, 16), 16)
-            total = carried[rows, cols(c)] + far_part[0, rows, cols(c)].astype(F32)
-            final[rows, cols(c)] = total.astype(BF16)
-
-        pltpu.make_async_copy(final.at[:, cols(c)], next_ref.at[:, cols(c)], final_sem).start()
-
-    drain(next_ref, final_sem)
 
     drain(carried, s_send.at[0])
 
@@ -571,32 +560,35 @@
                 drain(far_send.at[slot, r], cross_send.at[slot, r])
 
 
-def finish(next_ref, prev_ref, pin_ref, pout_ref, next_out, prev_out, gin_out, gout_out, sum_in, sum_out, sems):
-    own_h = sum_in.shape[0]
-    step = own_h // 4
-    moves = [
-        pltpu.make_async_copy(next_ref, next_out, sems.at[0]),
-        pltpu.make_async_copy(prev_ref, prev_out, sems.at[1]),
-    ]
-    for move in moves:
-        move.start()
-    for i, (part, total, out) in enumerate(((pin_ref, sum_in, gin_out), (pout_ref, sum_out, gout_out))):
-        @pl.loop(0, own_h // step)
+def finish(near_ref, far_ref, prev_ref, pin_ref, pout_ref, next_out, prev_out, gin_out, gout_out, total, sum_in, sum_out, sems):
+    move = pltpu.make_async_copy(prev_ref, prev_out, sems.at[1])
+    move.start()
+    for i, (part, whole, out) in enumerate(((pin_ref, sum_in, gin_out), (pout_ref, sum_out, gout_out))):
+        step = whole.shape[0] // 4
+
+        @pl.loop(0, 4)
         def _(b):
             @pl.loop(0, step // 16)
             def _(j):
                 rows = pl.ds(pl.multiple_of(b * step + j * 16, 16), 16)
-                total[rows, :] = functools.reduce(
+                whole[rows, :] = functools.reduce(
                     jnp.add, [part[k, rows, :].astype(F32) for k in range(part.shape[0])]
                 )
 
             block = pl.ds(pl.multiple_of(b * step, step), step)
-            pltpu.make_async_copy(total.at[block], out.at[block], sems.at[2 + i]).start()
-
-    for move in moves:
-        move.wait()
-    for i, (total, out) in enumerate(((sum_in, gin_out), (sum_out, gout_out))):
-        pltpu.make_async_copy(total, out, sems.at[2 + i]).wait()
+            pltpu.make_async_copy(whole.at[block], out.at[block], sems.at[2 + i]).start()
+
+    @pl.loop(0, total.shape[0] // 16)
+    def _(j):
+        rows = pl.ds(pl.multiple_of(j * 16, 16), 16)
+        total[rows, :] = (near_ref[rows, :] + far_ref[rows, :].astype(F32)).astype(BF16)
+
+    last = pltpu.make_async_copy(total, next_out, sems.at[0])
+    last.start()
+    move.wait()
+    for i, (whole, out) in enumerate(((sum_in, gin_out), (sum_out, gout_out))):
+        pltpu.make_async_copy(whole, out, sems.at[2 + i]).wait()
+    last.wait()
 
 
 def per_device(fwd_states, fwd_routes, bwd_states, bwd_routes, bwd_cot, w_in, w_out):
@@ -647,8 +639,6 @@
         pltpu.VMEM((q, max(ROWS, near * tail), near * ROWS), BF16),
         pltpu.VMEM((2, tokens, depth), F32),
         pltpu.VMEM((2, 2, tokens, depth), BF16),
-        pltpu.VMEM((2, tokens, depth), BF16),
-        pltpu.VMEM((tokens, depth), F32),
         pltpu.VMEM((tokens, depth), BF16),
         pltpu.VMEM((tokens, depth), BF16),
     ]
@@ -661,26 +651,29 @@
     operands = (fwd_states[0], fwd_routes[0].T, bwd_states[0], bwd_routes[0].T, bwd_cot[0], w_in[0], w_out[0])
     results = pl.pallas_call(
         functools.partial(kernel, experts, sections, main, tail),
-        out_shape=(states, states, parts, parts),
+        out_shape=(jax.ShapeDtypeStruct((tokens, depth), F32), states, states, parts, parts),
         in_specs=[pl.BlockSpec(memory_space=pltpu.HBM)] * 7,
-        out_specs=(anywhere,) * 4,
+        out_specs=(anywhere,) * 5,
         scratch_shapes=[
             *buffers,
             dma((5,)), dma((3,)), dma((3, 2, CHUNKS)), dma((2,)), dma((2, 2)), dma((3, 3)), dma((3, CHUNKS)),
             dma((2,)), dma((2,)), dma((2, CHUNKS, 3)), dma((2, 2)), dma((2, CHUNKS)),
-            dma((2,)), dma((2,)), dma((2,)), dma((2,)), dma((2,)), dma((1,)), dma((CHUNKS,)), dma, pltpu.SemaphoreType.REGULAR,
+            dma((2,)), dma((2,)), dma((2,)), dma((2,)), dma((2,)), dma((1,)), dma((CHUNKS,)), pltpu.SemaphoreType.REGULAR,
         ],
         compiler_params=pltpu.CompilerParams(
             collective_id=0, has_side_effects=True, vmem_limit_bytes=grant
         ),
     )(*(pltpu.with_memory_space_constraint(v, pltpu.HBM) for v in operands))
+    local = pl.BlockSpec(memory_space=pltpu.VMEM)
     outs = pl.pallas_call(
         finish,
         out_shape=(states, states, grads, grads),
-        in_specs=[anywhere] * 2 + [pl.BlockSpec(memory_space=pltpu.VMEM)] * 2,
+        in_specs=[local, local, anywhere, local, local],
         out_specs=(pl.BlockSpec(memory_space=pltpu.HBM),) * 4,
-        scratch_shapes=[pltpu.VMEM((own_h, depth), F32), pltpu.VMEM((own_h, depth), F32), dma((4,))],
-        compiler_params=pltpu.CompilerParams(vmem_limit_bytes=own_h * depth * 8 + 2 * 1024 * 1024),
+        scratch_shapes=[
+            pltpu.VMEM((tokens, depth), BF16), pltpu.VMEM((own_h, depth), F32), pltpu.VMEM((own_h, depth), F32), dma((4,)),
+        ],
+        compiler_params=pltpu.CompilerParams(vmem_limit_bytes=(8 * own_h + 2 * tokens) * depth + 2 * 1024 * 1024),
     )(*results)
     return tuple(out[None] for out in outs)
 

time: 121 us -> 121 us (level)
  no operation moved by 1% of the time
where the time goes in v4:
time: 121 us
  Pallas kernels  120 us (99%)
    pallas_call x1, Pallas kernels, per_device(): pl.pallas_call(functools.partial(kernel, experts, sections, main, tail),...  118 us

profile of v4, /device:TPU:15, one launch (start us, length us, event | category | flops | bytes accessed | tf_op | source)
XLA Modules:
  0.0 120.5 jit_solution(1303459494930462115)
XLA Ops:
  0.6 117.5 %shard_map.102 = (f32[128,2048]{1,0:T(8,128)S(1)}, bf16[128,2048]{1,0:T(8,128)(2,1)S(1)}, bf16[128,2048]{1,0:T(8,128)(2,1)S(1)}, bf16[2,256,2048]{2,1,0:T(8,128)(2,1)S(1)}, bf16[2,256,2048]{2,1,0:T(8,128)(2,1)S(1)}) custom-call(bf16[128,2048]{1,0:T(8,128)(2,1)} %bitcast.17, s32[2,128]{1,0:T(2,128)} %bitcast.20, bf16[128,2048]{1,0:T(8,128)(2,1)} %bitcast.18, ...), custom_call_target="tpu_custom_call" | custom-call | tf_op jit(solution)/shard_map/pallas_call | solution.py:652
  118.1 2.4 %shard_map.103 = (bf16[128,2048]{1,0:T(8,128)(2,1)}, bf16[128,2048]{1,0:T(8,128)(2,1)}, f32[256,2048]{1,0:T(8,128)}, f32[256,2048]{1,0:T(8,128)}) custom-call(f32[128,2048]{1,0:T(8,128)S(1)} %get-tuple-element.13.near_ref, bf16[128,2048]{1,0:T(8,128)(2,1)S(1)} %get-tuple-element.14.far_ref, bf16[128,2048]{1,0:T(8,128)(2,1)S(1)} %get-tuple-element.15.prev_ref, ...), custom_call_target="tpu_custom_call" | custom-call | tf_op jit(solution)/shard_map/pallas_call | solution.py:668
